TPU v7x, 32 devices: a whole 2x2x4 slice. The times are simulated.
32 devices in a mesh: groups: 2 (over x), mp: 8 (over z, y), psg: 2 (over core).
Axes of the slice: x: 2, y: 2, z: 4, core: 2. Of those that a mesh axis runs over, the one named last changes fastest.
Arguments:
- tokens: bfloat16 [512, 1024], P(('groups', 'mp', 'psg')), parts along dimension 0, may hold values from -6 to 6
- enc_gain: float32 [1024], replicated, may hold values from 0.25 to 1.75
- w_in: bfloat16 [1024, 32768], P(None, 'mp'), may hold values from -0.1875 to 0.1875
- w_out: bfloat16 [32768, 1024], P('mp'), may hold values from -0.046875 to 0.046875
- final_gain: float32 [1024], replicated, may hold values from 0.25 to 1.75
- w_keyval: bfloat16 [1024, 2, 16384], P(None, None, 'mp'), may hold values from -0.1875 to 0.1875
- answer_states: bfloat16 [256, 1024], P('groups'), parts along dimension 0, may hold values from -6 to 6
- dec_gain: float32 [1024], replicated, may hold values from 0.25 to 1.75
- w_query: bfloat16 [1024, 16384], P(None, 'mp')
- w_attn_out: bfloat16 [16384, 1024], P('mp'), may hold values from -0.046875 to 0.046875
- passage_lengths: int32 [32], P('groups'), parts along dimension 0, may hold values from 1 to 16
- passage_owner: int32 [32], P('groups'), parts along dimension 0, may hold values from 0 to 3, as said below
- answer_lengths: int32 [8], P('groups'), parts along dimension 0, may hold values from 1 to 64, 128 in all
Outputs:
- encoded: bfloat16 [512, 1024], P(('groups', 'mp', 'psg')), parts along dimension 0
- answer: bfloat16 [256, 1024], P(('groups', 'mp')), parts along dimension 0
There are 2 independent parts, one for each index of `groups`. A program takes and returns all parts, laid end to end along the dimension named above; an argument that names none is the same for every part. Nothing has to cross between parts.
Inputs may be any that keep to these rules, and one draw needn't show every extreme that they name: `passage_owner`: every one of the 4 questions owns at least one passage.
All inputs are finite; a program needn't handle non-finite values.
Results may differ from a plain program's by a relative error of at most 0.028.
Values may be sent and summed in bfloat16 or wider, within the bound.
A program may use at most 128 MiB of HBM per device.

v0:
```python
import jax
import jax.numpy as jnp
from jax import lax
from jax.sharding import PartitionSpec as P

DH = 128
P_SLOT = 16


eps = 1e-06


def merged(x, axis, combine):
    everything = jax.tree.map(lambda part: lax.all_gather(part, axis), x)
    initial = jax.tree.map(lambda part: part[0], everything)

    def step(k, so_far):
        return combine(so_far, jax.tree.map(lambda part: part[k], everything))

    return lax.fori_loop(1, lax.axis_size(axis), step, initial)


def norm_rows(states, gain):
    wide = states.astype(jnp.float32)
    factor = lax.rsqrt(jnp.mean(wide * wide, axis=-1, keepdims=True) + eps)
    return wide * factor * gain


def key_mask(token_index, passage_lengths, passage_owner, answer_lengths, answer_count):
    passage = token_index // P_SLOT
    place = token_index % P_SLOT
    count = passage_lengths.shape[0]
    match = passage[:, None] == jnp.arange(count, dtype=jnp.int32)[None, :]
    token_length = jnp.sum(jnp.where(match, passage_lengths[None, :], 0), axis=1)
    token_owner = jnp.sum(jnp.where(match, passage_owner[None, :], 0), axis=1)
    ends = jnp.cumsum(answer_lengths)
    answer_index = jnp.arange(answer_count, dtype=jnp.int32)
    question = jnp.sum((answer_index[:, None] >= ends[None, :]).astype(jnp.int32), axis=1)
    return (place < token_length)[None, :] & (token_owner[None, :] == question[:, None])


def attend_local(query, keys, values, allowed):
    scores = jnp.einsum("qhd,khd->hqk", query, keys, preferred_element_type=jnp.float32) * DH ** (
        -0.5
    )
    scores = jnp.where(allowed[None], scores, -1e30)
    top = jnp.max(scores, axis=2)
    weights = jnp.where(allowed[None], jnp.exp(scores - top[..., None]), 0.0)
    total = jnp.sum(weights, axis=2)
    summed = jnp.einsum(
        "hqk,khd->hqd", weights.astype(jnp.bfloat16), values, preferred_element_type=jnp.float32
    )
    return (top, total, summed)


def combine(left_part, right_part):
    left_top, left_total, left_sum = left_part
    right_top, right_total, right_sum = right_part
    new_top = jnp.maximum(left_top, right_top)
    left_factor = jnp.exp(left_top - new_top)
    right_factor = jnp.exp(right_top - new_top)
    new_total = left_total * left_factor + right_total * right_factor
    new_sum = left_sum * left_factor[..., None] + right_sum * right_factor[..., None]
    return (new_top, new_total, new_sum)


def per_device(
    tokens,
    enc_gain,
    w_in,
    w_out,
    final_gain,
    w_keyval,
    answer_states,
    dec_gain,
    w_query,
    w_attn_out,
    passage_lengths,
    passage_owner,
    answer_lengths,
):
    row_count = tokens.shape[0]
    model_width = tokens.shape[1]
    answer_count = answer_states.shape[0]
    mp_count = lax.axis_size("mp")
    psg_count = lax.axis_size("psg")
    mp_index = lax.axis_index("mp")
    psg_index = lax.axis_index("psg")
    head_local = w_query.shape[1] // DH
    inner_local = head_local * DH
    joined_weight = w_keyval.reshape(model_width, 2 * inner_local)
    normed = norm_rows(lax.all_gather(tokens, "mp", axis=0, tiled=True), enc_gain).astype(
        jnp.bfloat16
    )
    hidden = jnp.maximum(jnp.dot(normed, w_in, preferred_element_type=jnp.float32), 0.0).astype(
        jnp.bfloat16
    )
    partial_sums = jnp.dot(hidden, w_out, preferred_element_type=jnp.float32)
    own_rows = tokens.astype(jnp.float32)
    summed_rows = lax.psum_scatter(partial_sums, "mp", scatter_dimension=0, tiled=True)
    encoded = (own_rows + summed_rows).astype(jnp.bfloat16)
    memory = norm_rows(encoded, final_gain).astype(jnp.bfloat16)
    joined = jnp.dot(
        lax.all_gather(memory, "mp", axis=0, tiled=True),
        joined_weight,
        preferred_element_type=jnp.float32,
    ).astype(jnp.bfloat16)
    key_rows = joined.shape[0]
    keys = joined[:, :inner_local].reshape(key_rows, head_local, DH)
    values = joined[:, inner_local:].reshape(key_rows, head_local, DH)
    normed_answer = norm_rows(answer_states, dec_gain).astype(jnp.bfloat16)
    query = jnp.dot(normed_answer, w_query, preferred_element_type=jnp.float32).astype(jnp.bfloat16)
    query = query.reshape(answer_count, head_local, DH)
    local_index = jnp.arange(key_rows, dtype=jnp.int32)
    block = local_index // row_count
    token_index = (block * psg_count + psg_index) * row_count + local_index % row_count
    allowed = key_mask(token_index, passage_lengths, passage_owner, answer_lengths, answer_count)
    partial_attention = attend_local(query, keys, values, allowed)
    top, total, summed = merged(partial_attention, "psg", combine)
    context = (summed / total[..., None]).astype(jnp.bfloat16)
    context = context.transpose(1, 0, 2).reshape(answer_count, inner_local)
    out_count = answer_count // mp_count
    block = context
    result = lax.psum_scatter(
        jnp.dot(block, w_attn_out, preferred_element_type=jnp.float32),
        "mp",
        scatter_dimension=0,
        tiled=True,
    )
    own_answer = lax.dynamic_slice_in_dim(answer_states, mp_index * out_count, out_count, 0).astype(
        jnp.float32
    )
    return (encoded, (own_answer + result).astype(jnp.bfloat16))


def solution(mesh):
    placed = (
        P(("groups", "mp", "psg"), None),
        P(),
        P(None, "mp"),
        P("mp", None),
        P(),
        P(None, None, "mp"),
        P("groups", None),
        P(),
        P(None, "mp"),
        P("mp", None),
        P("groups"),
        P("groups"),
        P("groups"),
    )
    return jax.shard_map(
        per_device,
        mesh=mesh,
        in_specs=placed,
        out_specs=(P(("groups", "mp", "psg"), None), P(("groups", "mp"), None)),
        check_vma=False,
    )
```

profile of v0, /device:TPU:0, one launch (start us, length us, event | category | flops | bytes accessed | tf_op | source)
XLA Modules:
  0.0 240.3 jit_solution(5375088046361659702)
XLA Ops:
  7.2 0.0 reduce-scatter.3.cloned.1.call-start
  7.2 32.8 %all_gather.24 = bf16[128,1024]{1,0:T(8,128)(2,1)S(1)} all-gather(bf16[16,1024]{1,0:T(8,128)(2,1)} %param.13), channel_id=1, replica_groups=mesh['groups'=2,'mp'=8,'psg'=2] {'mp'}, dimensions={0}, use_global_device_ids=true | all-gather | bytes 294912 | tf_op jit(solution)/shard_map/all_gather | solution.py:92
  40.0 0.1 fusion.6
  40.1 0.0 copy-start.1
  40.1 0.0 copy-start.8
  40.1 0.0 copy-start.6
  40.2 0.0 copy-start.7
  40.2 9.1 %fusion.5 = f32[128,1024]{1,0:T(8,128)} fusion(bf16[4096,1024]{1,0:T(8,128)(2,1)} %param.16, bf16[1024,4096]{1,0:T(8,128)(2,1)} %param.15, bf16[128,1024]{1,0:T(8,128)(2,1)S(1)} %all_gather.24, f32[1024]{0:T(1024)} %param.14, f32[128]{0:T(128)S(1)} %add_rsqrt_fusion.2), kind=kOutput, calls=%fused_computation.11 | convolution fusion | flops 2149056512 | bytes 17568256 | tf_op jit(solution)/shard_map/dot_general | solution.py:98
  49.2 0.0 reduce-scatter.3.cloned.1.call-update
  49.3 0.0 all-gather.5.cloned.1.call-start
  49.3 0.0 copy-done.1
  49.3 0.1 fusion.9
  49.5 0.0 copy-done.8
  49.5 0.2 reduce-window.8
  49.7 0.0 copy-done.6
  49.7 0.0 copy-done.7
  49.7 0.1 select_reduce_fusion.1
  49.8 0.1 convert_reduce_fusion
  49.8 0.0 copy-start
  49.8 0.0 copy-start.5
  49.8 0.0 copy-start.2
  49.9 0.0 copy-start.4
  49.9 12.2 %copy.42 = bf16[128,8,2,2048]{3,1,2,0:T(8,128)(2,1)} copy(bf16[128,8,2,2048]{3,2,1,0:T(2,128)(2,1)} %bitcast.34) | data formatting | bytes 16777216
  62.1 0.1 compare_and_fusion
  62.2 0.0 copy-done
  62.2 0.0 copy-done.5
  62.2 0.8 fusion.2
  63.0 50.1 %reduce-scatter.3.cloned.1.call-done = f32[16,1024]{1,0:T(8,128)} async-done(((f32[128,1024]{1,0:T(8,128)}), f32[16,1024]{1,0:T(8,128)}) %reduce-scatter.3.cloned.1.call-update) | async-done | bytes 65552 | tf_op jit(solution)/shard_map/reduce_scatter | solution.py:100
  113.1 0.0 copy-done.2
  113.1 1.0 fusion.32
  114.1 0.0 copy-start.3
  114.1 0.0 copy-done.4
  114.1 0.1 fusion.34
  114.2 31.0 %all_gather.25 = bf16[128,1024]{1,0:T(8,128)(2,1)S(1)} all-gather(bf16[16,1024]{1,0:T(8,128)(2,1)S(1)} %fusion.34), channel_id=1, replica_groups=mesh['groups'=2,'mp'=8,'psg'=2] {'mp'}, dimensions={0}, use_global_device_ids=true | all-gather | bytes 294912 | tf_op jit(solution)/shard_map/all_gather | solution.py:104
  145.2 4.6 %convolution_convert_fusion = bf16[128,4096]{1,0:T(8,128)(2,1)S(1)} fusion(bf16[128,1024]{1,0:T(8,128)(2,1)S(1)} %all_gather.25, bf16[1024,4096]{1,0:T(8,128)(2,1)} %bitcast.33), kind=kOutput, calls=%fused_computation.2 | convolution fusion | flops 1074266112 | bytes 9699328 | tf_op jit(solution)/shard_map/dot_general | solution.py:103
  149.8 0.1 slice_bitcast_fusion
  149.9 0.5 fusion.48
  150.5 0.0 copy-done.3
  150.5 1.4 fusion.12
  151.9 0.0 all-gather.5.cloned.1.call-update
  151.9 0.0 reduce-scatter.5.cloned.1.call-start
  151.9 1.8 all-gather.1
  153.8 0.2 fusion.3
  154.0 1.8 all-gather.2
  155.8 5.8 %all-gather.5.cloned.1.call-done = f32[32,128,128]{2,1,0:T(8,128)} async-done(((f32[16,128,128]{2,1,0:T(8,128)}), f32[32,128,128]{2,1,0:T(8,128)}) %all-gather.5.cloned.1.call-update) | async-done | bytes 2097168 | tf_op jit(solution)/shard_map/all_gather | solution.py:14
  161.5 1.7 fusion.47
  163.2 0.3 copy.38
  163.6 0.3 copy.37
  163.9 0.2 divide_convert_fusion
  164.1 3.7 %fusion.49 = f32[128,1024]{1,0:T(8,128)} fusion(bf16[128,2048]{0,1:T(8,128)(2,1)S(1)} %bitcast.35, bf16[2048,1024]{1,0:T(8,128)(2,1)} %param.22), kind=kOutput, calls=%fused_computation.80 | convolution fusion | flops 536870912 | bytes 5242880 | tf_op jit(solution)/shard_map/dot_general | solution.py:125
  167.9 0.0 reduce-scatter.5.cloned.1.call-update
  167.9 64.4 %reduce-scatter.5.cloned.1.call-done = f32[16,1024]{1,0:T(8,128)} async-done(((f32[128,1024]{1,0:T(8,128)}), f32[16,1024]{1,0:T(8,128)}) %reduce-scatter.5.cloned.1.call-update) | async-done | bytes 65552 | tf_op jit(solution)/shard_map/reduce_scatter | solution.py:124
  232.3 1.5 add_convert_fusion
  (6 shorter events, 0.1 us)
Async XLA Ops:
  7.2 105.9 %reduce-scatter.3.cloned.1.call-start = ((), (), s32[]{:S(2)}) async-start(), calls=%async_computation.2 | async-start | bytes 589824 | tf_op jit(solution)/shard_map/reduce_scatter | solution.py:100
  40.1 9.2 %copy-start.1 = (bf16[128,1024]{1,0:T(8,128)(2,1)S(1)}, bf16[128,1024]{1,0:T(8,128)(2,1)}, u32[]{:S(2)}) copy-start(bf16[128,1024]{1,0:T(8,128)(2,1)} %param.19) | copy-start | bytes 786436
  40.1 9.4 %copy-start.8 = (s32[4]{0:T(128)S(1)}, s32[4]{0:T(128)}, u32[]{:S(2)}) copy-start(s32[4]{0:T(128)} %param.25) | copy-start | bytes 52
  40.1 9.5 %copy-start.6 = (s32[16]{0:T(128)S(1)}, s32[16]{0:T(128)}, u32[]{:S(2)}) copy-start(s32[16]{0:T(128)} %param.23) | copy-start | bytes 196
  40.2 9.5 %copy-start.7 = (s32[16]{0:T(128)S(1)}, s32[16]{0:T(128)}, u32[]{:S(2)}) copy-start(s32[16]{0:T(128)} %param.24) | copy-start | bytes 196
  49.3 112.3 %all-gather.5.cloned.1.call-start = ((), (), s32[]{:S(2)}) async-start(), calls=%async_computation.4 | async-start | bytes 3145728 | tf_op jit(solution)/shard_map/all_gather | solution.py:14
  49.8 12.4 %copy-start = (bf16[1024,2048]{1,0:T(8,128)(2,1)S(1)}, bf16[1024,2048]{1,0:T(8,128)(2,1)}, u32[]{:S(2)}) copy-start(bf16[1024,2048]{1,0:T(8,128)(2,1)} %param.21) | copy-start | bytes 12582916
  49.8 12.4 %copy-start.5 = (f32[1024]{0:T(1024)S(1)}, f32[1024]{0:T(1024)}, u32[]{:S(2)}) copy-start(f32[1024]{0:T(1024)} %param.20) | copy-start | bytes 12292
  49.8 63.3 %copy-start.2 = (bf16[16,1024]{1,0:T(8,128)(2,1)S(1)}, bf16[16,1024]{1,0:T(8,128)(2,1)}, u32[]{:S(2)}) copy-start(bf16[16,1024]{1,0:T(8,128)(2,1)} %param.13) | copy-start | bytes 98308
  49.9 64.2 %copy-start.4 = (f32[1024]{0:T(1024)S(1)}, f32[1024]{0:T(1024)}, u32[]{:S(2)}) copy-start(f32[1024]{0:T(1024)} %param.17) | copy-start | bytes 12292
  114.1 36.4 %copy-start.3 = (bf16[16,1024]{1,0:T(8,128)(2,1)}, bf16[16,1024]{1,0:T(8,128)(2,1)S(1)}, u32[]{:S(2)}) copy-start(bf16[16,1024]{1,0:T(8,128)(2,1)S(1)} %get-tuple-element.32) | copy-start | bytes 98308
  151.9 80.4 %reduce-scatter.5.cloned.1.call-start = ((), (), s32[]{:S(2)}) async-start(), calls=%async_computation.3 | async-start | bytes 589824 | tf_op jit(solution)/shard_map/reduce_scatter | solution.py:124
Sparse Core Ops, SparseCore 0:
  49.4 63.6 reduce-scatter.2
  152.0 9.4 all-gather.4
  168.0 64.2 reduce-scatter.4
where the time goes:
time: 241 us; the launch traced here: 240 us
  waiting for transfers between devices  120 us (50%)
  blocking collectives  67.4 us (28%)
  matrix products  20.2 us (8%)
  local copies, waits for them, and re-layouts  14.7 us (6%)
  between operations  13.9 us (6%)
  other arithmetic  3.72 us (2%)
    reduce_scatter x1, waiting for transfers between devices, per_device(): lax.psum_scatter(jnp.dot(block, w_attn_out, preferred_element_type=jnp.fl...  64.4 us
    reduce_scatter x1, waiting for transfers between devices, per_device(): lax.psum_scatter(partial_sums, 'mp', scatter_dimension=0, tiled=True)  50.1 us
    all_gather x1, blocking collectives, per_device(): lax.all_gather(tokens, 'mp', axis=0, tiled=True)  32.8 us
    all_gather x1, blocking collectives, per_device(): lax.all_gather(memory, 'mp', axis=0, tiled=True)  31 us
    unnamed x22, local copies, waits for them, and re-layouts  13 us
    dot_general x1, matrix products, per_device(): partial_sums = jnp.dot(hidden, w_out, preferred_element_type=jnp.float32)  9.08 us
    all_gather x1, waiting for transfers between devices, merged(): everything = jax.tree.map(lambda part: lax.all_gather(part, axis), x)  5.75 us
  transfers between devices with their start and end apart: 3, of which 3 were waited for; matrix products, arithmetic and copies ran while one was open for 6% of the time, Pallas kernels for 0%

commit v1 on v0

v1 whole, which is shorter than its diff:
```python
import functools

import jax
import jax.numpy as jnp
from jax import lax
from jax.experimental import pallas as pl
from jax.experimental.pallas import tpu as pltpu
from jax.sharding import PartitionSpec as P

DH = 128
P_SLOT = 16
EPS = 1e-06
MESH = pl.DeviceIdType.MESH
F32 = jnp.float32
BF16 = jnp.bfloat16


def norm_rows(states, gain):
    wide = states.astype(F32)
    factor = lax.rsqrt(jnp.mean(wide * wide, axis=-1, keepdims=True) + EPS)
    return wide * factor * gain


def tile_of(width, most):
    tile = min(width, most)
    while width % tile:
        tile //= 2
    return tile


def kernel(
    n,
    cores,
    tokens_ref,
    enc_gain_ref,
    final_gain_ref,
    dec_gain_ref,
    answers_ref,
    own_answers_ref,
    lengths_ref,
    owner_ref,
    rows_ref,
    w_in_hbm,
    w_out_hbm,
    w_kv_hbm,
    w_query_hbm,
    w_proj_hbm,
    encoded_ref,
    answer_ref,
    w_in,
    w_out,
    w_kv,
    w_query,
    w_proj,
    normed_all,
    hidden,
    part,
    send1,
    recv1,
    memory_all,
    keys,
    values,
    query,
    context,
    part2,
    send2,
    recv2,
    final_all,
    load_sem,
    ag_send,
    ag_recv,
    rs_send,
    rs_recv,
    mem_send,
    mem_recv,
    fwd_send,
    fwd_recv,
    rs2_send,
    rs2_recv,
    fin_send,
    fin_recv,
):
    me = lax.axis_index("mp")
    core = lax.axis_index("psg")
    rows, width = tokens_ref.shape
    hidden_count = w_in.shape[1]
    inner = w_query.shape[1]
    answer_count = answers_ref.shape[0]
    out_count = answer_count // n
    chunks1, chunks2 = send1.shape[0], send2.shape[0]
    chunk1, chunk2 = send1.shape[-1], send2.shape[-1]

    first = pl.multiple_of(core * inner, inner)
    loads = [
        pltpu.make_async_copy(w_query_hbm.at[:, pl.ds(first, inner)], w_query, load_sem.at[0]),
        pltpu.make_async_copy(w_in_hbm, w_in, load_sem.at[1]),
        pltpu.make_async_copy(w_out_hbm, w_out, load_sem.at[2]),
        pltpu.make_async_copy(w_kv_hbm, w_kv, load_sem.at[3]),
        pltpu.make_async_copy(w_proj_hbm.at[pl.ds(first, inner), :], w_proj, load_sem.at[4]),
    ]
    for load in loads:
        load.start()

    barrier = pltpu.get_barrier_semaphore()
    peers = [lax.rem(me + k, n) for k in range(1, n)]
    others = [lax.rem(core + k, cores) for k in range(1, cores)]
    for peer in peers:
        pl.semaphore_signal(barrier, inc=1, device_id={"mp": peer}, device_id_type=MESH)
    for other in others:
        pl.semaphore_signal(barrier, inc=1, device_id={"psg": other}, device_id_type=MESH)
    normed_all[me] = norm_rows(tokens_ref[...], enc_gain_ref[...]).astype(BF16)
    pl.semaphore_wait(barrier, n - 1 + cores - 1)

    def to_peer(src, dst, send_sem, recv_sem, peer):
        return pltpu.make_async_remote_copy(
            src_ref=src, dst_ref=dst, send_sem=send_sem, recv_sem=recv_sem,
            device_id={"mp": peer}, device_id_type=MESH,
        )

    def to_core(src, dst, send_sem, recv_sem, other):
        return pltpu.make_async_remote_copy(
            src_ref=src, dst_ref=dst, send_sem=send_sem, recv_sem=recv_sem,
            device_id={"psg": other}, device_id_type=MESH,
        )

    def gather_copy(source, k, peer):
        return to_peer(normed_all.at[source], normed_all.at[source], ag_send.at[k], ag_recv.at[source], peer)

    for k, peer in enumerate(peers):
        gather_copy(me, k, peer).start()

    normed_answer = norm_rows(answers_ref[...], dec_gain_ref[...]).astype(BF16)
    loads[0].wait()
    q_tile = tile_of(inner, 512)

    def query_step(i, carry):
        at = pl.ds(pl.multiple_of(i * q_tile, q_tile), q_tile)
        query[:, at] = jnp.dot(normed_answer, w_query[:, at], preferred_element_type=F32).astype(BF16)
        return carry

    lax.fori_loop(0, inner // q_tile, query_step, 0)

    loads[1].wait()
    for k, peer in enumerate(peers):
        gather_copy(peer, k, peer).wait_recv()
    for k, peer in enumerate(peers):
        gather_copy(me, k, peer).wait_send()

    normed = normed_all[...].reshape(n * rows, width)
    h_tile = tile_of(hidden_count, 512)

    def hidden_step(i, carry):
        at = pl.ds(pl.multiple_of(i * h_tile, h_tile), h_tile)
        product = jnp.dot(normed, w_in[:, at], preferred_element_type=F32)
        hidden[:, at] = jnp.maximum(product, 0.0).astype(BF16)
        return carry

    lax.fori_loop(0, hidden_count // h_tile, hidden_step, 0)
    loads[2].wait()

    def sum_copy(c, source, k, peer):
        return to_peer(
            send1.at[c, peer], recv1.at[c, source], rs_send.at[c, k], rs_recv.at[c, source], peer
        )

    def out_step(c, carry):
        at = pl.ds(pl.multiple_of(c * chunk1, chunk1), chunk1)
        product = jnp.dot(hidden[...], w_out[:, at], preferred_element_type=F32)
        product = product.reshape(n, rows, chunk1)
        part[c] = product
        send1[c] = product.astype(BF16)
        for k, peer in enumerate(peers):
            sum_copy(c, me, k, peer).start()
        return carry

    lax.fori_loop(0, chunks1, out_step, 0)

    for c in range(chunks1):
        at = slice(c * chunk1, (c + 1) * chunk1)
        total = part[c, me]
        for k, peer in enumerate(peers):
            sum_copy(c, peer, k, peer).wait_recv()
            total = total + recv1[c, peer].astype(F32)
        encoded_ref[:, at] = (tokens_ref[:, at].astype(F32) + total).astype(BF16)
    memory_all[0, me] = norm_rows(encoded_ref[...], final_gain_ref[...]).astype(BF16)

    def memory_copy(source, k, peer):
        return to_peer(
            memory_all.at[0, source], memory_all.at[0, source], mem_send.at[k], mem_recv.at[source], peer
        )

    def forward_copy(source, s, other):
        return to_core(
            memory_all.at[0, source], memory_all.at[cores - s, source],
            fwd_send.at[s - 1, source], fwd_recv.at[cores - s - 1, source], other,
        )

    for k, peer in enumerate(peers):
        memory_copy(me, k, peer).start()
    for s, other in enumerate(others, 1):
        forward_copy(me, s, other).start()
    for c in range(chunks1):
        for k, peer in enumerate(peers):
            sum_copy(c, me, k, peer).wait_send()
    loads[3].wait()
    loads[4].wait()

    half = n * rows
    count = cores * half
    place_at = lax.broadcasted_iota(jnp.int32, (1, count), 1)
    slot = place_at // half
    block = (place_at % half) // rows
    token = (block * cores + (core + slot) % cores) * rows + place_at % rows
    passage = token // P_SLOT
    token_length = jnp.zeros((1, count), jnp.int32)
    token_owner = jnp.zeros((1, count), jnp.int32)
    for i in range(lengths_ref.shape[0]):
        token_length = jnp.where(passage == i, lengths_ref[i], token_length)
        token_owner = jnp.where(passage == i, owner_ref[i], token_owner)
    answer_at = lax.broadcasted_iota(jnp.int32, (answer_count, 1), 0)
    question = jnp.zeros((answer_count, 1), jnp.int32)
    end = jnp.int32(0)
    for i in range(rows_ref.shape[0]):
        end = end + rows_ref[i]
        question = question + jnp.where(answer_at >= end, 1, 0)
    token_key = jnp.where(token % P_SLOT < token_length, token_owner, -1)
    allowed = token_key == question

    for k, peer in enumerate(peers):
        memory_copy(peer, k, peer).wait_recv()
        for s, other in enumerate(others, 1):
            forward_copy(peer, s, other).start()

    k_tile = tile_of(inner, 512)

    def project(s):
        memory = memory_all[s].reshape(half, width)

        def step(i, carry):
            at = pl.ds(pl.multiple_of(i * k_tile, k_tile), k_tile)
            keys[s, :, at] = jnp.dot(memory, w_kv[0, :, at], preferred_element_type=F32).astype(BF16)
            values[s, :, at] = jnp.dot(memory, w_kv[1, :, at], preferred_element_type=F32).astype(BF16)
            return carry

        lax.fori_loop(0, inner // k_tile, step, 0)

    project(0)
    for s, other in enumerate(others, 1):
        for source in [me] + peers:
            pltpu.make_async_remote_copy(
                src_ref=memory_all.at[0, source], dst_ref=memory_all.at[s, source],
                send_sem=fwd_send.at[s - 1, source], recv_sem=fwd_recv.at[s - 1, source],
                device_id={"psg": other}, device_id_type=MESH,
            ).wait_recv()
        project(s)

    for h in range(inner // DH):
        at = slice(h * DH, (h + 1) * DH)
        head_keys = keys[:, :, at].reshape(count, DH)
        head_values = values[:, :, at].reshape(count, DH)
        scores = lax.dot_general(
            query[:, at], head_keys, (((1,), (1,)), ((), ())), preferred_element_type=F32
        ) * DH ** (-0.5)
        scores = jnp.where(allowed, scores, -1e30)
        top = jnp.max(scores, axis=1, keepdims=True)
        weights = jnp.where(allowed, jnp.exp(scores - top), 0.0)
        total = jnp.sum(weights, axis=1, keepdims=True)
        summed = jnp.dot(weights.astype(BF16), head_values, preferred_element_type=F32)
        context[:, at] = (summed / total).astype(BF16)

    def sum2_copy(c, source, k, peer):
        return to_peer(
            send2.at[c, peer], recv2.at[c, source], rs2_send.at[c, k], rs2_recv.at[c, source], peer
        )

    for c in range(chunks2):
        product = jnp.dot(
            context[...], w_proj[:, c * chunk2 : (c + 1) * chunk2], preferred_element_type=F32
        )
        for j in range(n):
            block_rows = product[j * out_count : (j + 1) * out_count]
            part2[c, j] = block_rows
            send2[c, j] = block_rows.astype(BF16)
        for k, peer in enumerate(peers):
            sum2_copy(c, me, k, peer).start()

    for k, peer in enumerate(peers):
        memory_copy(me, k, peer).wait_send()
    for s, other in enumerate(others, 1):
        for source in [me] + peers:
            forward_copy(source, s, other).wait_send()

    for c in range(chunks2):
        total = part2[c, me]
        for k, peer in enumerate(peers):
            sum2_copy(c, peer, k, peer).wait_recv()
            total = total + recv2[c, peer].astype(F32)
        final_all[0, :, c * chunk2 : (c + 1) * chunk2] = total

    def final_copy(s, other):
        return to_core(
            final_all.at[0], final_all.at[cores - s], fin_send.at[s - 1], fin_recv.at[cores - s - 1], other
        )

    for s, other in enumerate(others, 1):
        final_copy(s, other).start()
    for c in range(chunks2):
        for k, peer in enumerate(peers):
            sum2_copy(c, me, k, peer).wait_send()
    total = final_all[0]
    for s, other in enumerate(others, 1):
        pltpu.make_async_remote_copy(
            src_ref=final_all.at[0], dst_ref=final_all.at[s],
            send_sem=fin_send.at[s - 1], recv_sem=fin_recv.at[s - 1],
            device_id={"psg": other}, device_id_type=MESH,
        ).wait_recv()
        total = total + final_all[s]
    answer_ref[...] = (own_answers_ref[me].astype(F32) + total).astype(BF16)
    for s, other in enumerate(others, 1):
        final_copy(s, other).wait_send()


def per_device(
    n,
    cores,
    tokens,
    enc_gain,
    w_in,
    w_out,
    final_gain,
    w_keyval,
    answer_states,
    dec_gain,
    w_query,
    w_attn_out,
    passage_lengths,
    passage_owner,
    answer_lengths,
):
    rows, width = tokens.shape
    hidden_count = w_in.shape[1]
    inner = w_query.shape[1] // cores
    answer_count = answer_states.shape[0]
    out_count = answer_count // n
    half = n * rows
    chunk1 = tile_of(width, 256)
    chunk2 = tile_of(width, 512)
    chunks1, chunks2 = width // chunk1, width // chunk2
    core = lax.axis_index("psg")
    w_kv = lax.dynamic_slice_in_dim(w_keyval, core * inner, inner, 2).transpose(1, 0, 2)
    vmem = pl.BlockSpec(memory_space=pltpu.VMEM)
    smem = pl.BlockSpec(memory_space=pltpu.SMEM)
    hbm = pl.BlockSpec(memory_space=pl.ANY)
    dma = pltpu.SemaphoreType.DMA
    others = max(cores - 1, 1)
    return pl.pallas_call(
        functools.partial(kernel, n, cores),
        out_shape=(
            jax.ShapeDtypeStruct((rows, width), BF16),
            jax.ShapeDtypeStruct((out_count, width), BF16),
        ),
        in_specs=[vmem] * 6 + [smem] * 3 + [hbm] * 5,
        out_specs=(vmem, vmem),
        scratch_shapes=[
            pltpu.VMEM((width, hidden_count), BF16),
            pltpu.VMEM((hidden_count, width), BF16),
            pltpu.VMEM((2, width, inner), BF16),
            pltpu.VMEM((width, inner), BF16),
            pltpu.VMEM((inner, width), BF16),
            pltpu.VMEM((n, rows, width), BF16),
            pltpu.VMEM((half, hidden_count), BF16),
            pltpu.VMEM((chunks1, n, rows, chunk1), F32),
            pltpu.VMEM((chunks1, n, rows, chunk1), BF16),
            pltpu.VMEM((chunks1, n, rows, chunk1), BF16),
            pltpu.VMEM((cores, n, rows, width), BF16),
            pltpu.VMEM((cores, half, inner), BF16),
            pltpu.VMEM((cores, half, inner), BF16),
            pltpu.VMEM((answer_count, inner), BF16),
            pltpu.VMEM((answer_count, inner), BF16),
            pltpu.VMEM((chunks2, n, out_count, chunk2), F32),
            pltpu.VMEM((chunks2, n, out_count, chunk2), BF16),
            pltpu.VMEM((chunks2, n, out_count, chunk2), BF16),
            pltpu.VMEM((cores, out_count, width), F32),
            dma((5,)),
            dma((n,)),
            dma((n,)),
            dma((chunks1, n)),
            dma((chunks1, n)),
            dma((n,)),
            dma((n,)),
            dma((others, n)),
            dma((others, n)),
            dma((chunks2, n)),
            dma((chunks2, n)),
            dma((others,)),
            dma((others,)),
        ],
        compiler_params=pltpu.CompilerParams(
            collective_id=0, has_side_effects=True, vmem_limit_bytes=58 * 1024 * 1024
        ),
    )(
        tokens,
        enc_gain.reshape(1, width),
        final_gain.reshape(1, width),
        dec_gain.reshape(1, width),
        answer_states,
        answer_states.reshape(n, out_count, width),
        passage_lengths,
        passage_owner,
        answer_lengths,
        w_in,
        w_out,
        w_kv,
        w_query,
        w_attn_out,
    )


def solution(mesh):
    placed = (
        P(("groups", "mp", "psg"), None),
        P(),
        P(None, "mp"),
        P("mp", None),
        P(),
        P(None, None, "mp"),
        P("groups", None),
        P(),
        P(None, "mp"),
        P("mp", None),
        P("groups"),
        P("groups"),
        P("groups"),
    )
    return jax.shard_map(
        functools.partial(per_device, mesh.shape["mp"], mesh.shape["psg"]),
        mesh=mesh,
        in_specs=placed,
        out_specs=(P(("groups", "mp", "psg"), None), P(("groups", "mp"), None)),
        check_vma=False,
    )
```

time: 241 us -> 56.6 us (0.23)
  waiting for transfers between devices: 120 us -> 0 us
  blocking collectives: 67.4 us -> 0 us
  Pallas kernels: 0 us -> 44.5 us
  matrix products: 20.2 us -> 0 us
  between operations: 13.9 us -> 0.65 us
  other arithmetic: 3.72 us -> 0 us
  local copies, waits for them, and re-layouts: 14.7 us -> 11.1 us
    reduce_scatter x2 -> x0, waiting for transfers between devices: 114 us -> none  [the longest x1 64.4 us: per_device(): lax.psum_scatter(jnp.dot(block, w_attn_out, preferred_element_type=jnp.fl...]
    all_gather x4 -> x0, blocking collectives: 67.4 us -> none  [the longest x1 32.8 us: per_device(): lax.all_gather(tokens, 'mp', axis=0, tiled=True)]
    pallas_call x0 -> x1, Pallas kernels: none -> 44.5 us  [per_device(): pl.pallas_call(functools.partial(kernel, n, cores), out_shape=(jax.ShapeD...]
    dot_general x6 -> x0, matrix products: 20.2 us -> none  [the longest x1 9.08 us: per_device(): partial_sums = jnp.dot(hidden, w_out, preferred_element_type=jnp.float32)]
    unnamed x22 -> x3, local copies, waits for them, and re-layouts: 13 us -> 6 us
    all_gather x1 -> x0, waiting for transfers between devices: 5.75 us -> none  [merged(): everything = jax.tree.map(lambda part: lax.all_gather(part, axis), x)]
    dynamic_slice x0 -> x1, local copies, waits for them, and re-layouts: none -> 5.07 us  [per_device(): lax.dynamic_slice_in_dim(w_keyval, core * inner, inner, 2)]
  transfers between devices with their start and end apart: 3 -> 0, of which waited for: 3 -> 0; matrix products, arithmetic and copies ran while one was open for 6% -> 0% of each run, Pallas kernels for 0% -> 0%
where the time goes in v1:
time: 56.6 us; the launch traced here: 56.2 us
  Pallas kernels  44.5 us (79%)
  local copies, waits for them, and re-layouts  11.1 us (20%)
  between operations  0.65 us (1%)
    pallas_call x1, Pallas kernels, per_device(): pl.pallas_call(functools.partial(kernel, n, cores), out_shape=(jax.ShapeD...  44.5 us
    unnamed x3, local copies, waits for them, and re-layouts  6 us
    dynamic_slice x1, local copies, waits for them, and re-layouts, per_device(): lax.dynamic_slice_in_dim(w_keyval, core * inner, inner, 2)  5.07 us

profile of v1, /device:TPU:0, one launch (start us, length us, event | category | flops | bytes accessed | tf_op | source)
XLA Modules:
  0.0 56.2 jit_solution(18360281223574479405)
XLA Ops:
  0.6 5.1 %constant_dynamic-slice_fusion = bf16[1024,2,1024]{2,1,0:T(2,128)(2,1)S(1)} fusion(bf16[1024,2,2048]{2,1,0:T(2,128)(2,1)} %param.18, s32[]{:T(128)S(6)} %select_n.3), kind=kLoop, calls=%fused_computation.1 | loop fusion | bytes 8388612 | tf_op jit(solution)/shard_map/dynamic_slice | solution.py:350
  5.7 3.2 %copy.18 = bf16[1024,2,1024]{2,0,1:T(8,128)(2,1)} copy(bf16[1024,2,1024]{2,1,0:T(2,128)(2,1)S(1)} %constant_dynamic-slice_fusion) | data formatting | bytes 8388608
  9.0 44.5 %shard_map.140 = (bf16[16,1024]{1,0:T(8,128)(2,1)}, bf16[16,1024]{1,0:T(8,128)(2,1)}) custom-call(bf16[16,1024]{1,0:T(8,128)(2,1)} %tokens_ref.1, f32[1,1024]{1,0:T(1,128)} %bitcast.9, f32[1,1024]{1,0:T(1,128)} %bitcast.10, f32[1,1024]{1,0:T(1,128)} %bitcast.11, bf16[128,1024]{1,0:T(8,128)(2,1)} %answers_ref.1, bf16[8,16,1024]{2,1,0:T(8,128)(2,1)} %bitcast.8, ...), custom_call_target="tpu_custom_call" | custom-call | tf_op jit(solution)/shard_map/pallas_call | solution.py:356
  53.5 1.4 %copy.21 = bf16[16,1024]{1,0:T(8,128)(2,1)} copy(bf16[16,1024]{1,0:T(8,128)(2,1)} %get-tuple-element.4) | data formatting | bytes 65536
  54.9 1.4 %copy.22 = bf16[16,1024]{1,0:T(8,128)(2,1)} copy(bf16[16,1024]{1,0:T(8,128)(2,1)} %get-tuple-element.5) | data formatting | bytes 65536

commit v2 on v1

--- a/solution.py
+++ b/solution.py
@@ -26,6 +26,22 @@
     while width % tile:
         tile //= 2
     return tile
+
+
+def flipped(index, mask):
+    out, bit = index, 1
+    while bit <= mask:
+        if mask & bit:
+            out = out + bit * (1 - 2 * ((index // bit) % 2))
+        bit *= 2
+    return out
+
+
+def peers_of(index, count):
+    if count & (count - 1):
+        return [lax.rem(index + k, count) for k in range(1, count)]
+    order = sorted(range(1, count), key=lambda k: (-(k.bit_length()), k))
+    return [flipped(index, k) for k in order]
 
 
 def kernel(
@@ -49,6 +65,7 @@
     answer_ref,
     w_in,
     w_out,
+    kv_pairs,
     w_kv,
     w_query,
     w_proj,
@@ -62,6 +79,8 @@
     values,
     query,
     context,
+    pre_send,
+    pre_recv,
     part2,
     send2,
     recv2,
@@ -75,6 +94,8 @@
     mem_recv,
     fwd_send,
     fwd_recv,
+    pre_ssem,
+    pre_rsem,
     rs2_send,
     rs2_recv,
     fin_send,
@@ -87,22 +108,23 @@
     inner = w_query.shape[1]
     answer_count = answers_ref.shape[0]
     out_count = answer_count // n
-    chunks1, chunks2 = send1.shape[0], send2.shape[0]
-    chunk1, chunk2 = send1.shape[-1], send2.shape[-1]
+    chunks1, chunk1 = send1.shape[0], send1.shape[-1]
 
     first = pl.multiple_of(core * inner, inner)
     loads = [
         pltpu.make_async_copy(w_query_hbm.at[:, pl.ds(first, inner)], w_query, load_sem.at[0]),
+        pltpu.make_async_copy(w_kv_hbm.at[:, :, pl.ds(first, inner)], kv_pairs, load_sem.at[3]),
         pltpu.make_async_copy(w_in_hbm, w_in, load_sem.at[1]),
         pltpu.make_async_copy(w_out_hbm, w_out, load_sem.at[2]),
-        pltpu.make_async_copy(w_kv_hbm, w_kv, load_sem.at[3]),
         pltpu.make_async_copy(w_proj_hbm.at[pl.ds(first, inner), :], w_proj, load_sem.at[4]),
     ]
     for load in loads:
         load.start()
 
     barrier = pltpu.get_barrier_semaphore()
-    peers = [lax.rem(me + k, n) for k in range(1, n)]
+    peers = peers_of(me, n)
+    pair = me + 1 - 2 * (me % 2)
+    line = [2 * place + me % 2 for place in peers_of(me // 2, n // 2)]
     others = [lax.rem(core + k, cores) for k in range(1, cores)]
     for peer in peers:
         pl.semaphore_signal(barrier, inc=1, device_id={"mp": peer}, device_id_type=MESH)
@@ -123,11 +145,12 @@
             device_id={"psg": other}, device_id_type=MESH,
         )
 
-    def gather_copy(source, k, peer):
-        return to_peer(normed_all.at[source], normed_all.at[source], ag_send.at[k], ag_recv.at[source], peer)
-
-    for k, peer in enumerate(peers):
-        gather_copy(me, k, peer).start()
+    def gather_copy(source, slot, peer):
+        return to_peer(normed_all.at[source], normed_all.at[source], ag_send.at[slot], ag_recv.at[source], peer)
+
+    for peer in line:
+        gather_copy(me, peer, peer).start()
+    gather_copy(me, pair, pair).start()
 
     normed_answer = norm_rows(answers_ref[...], dec_gain_ref[...]).astype(BF16)
     loads[0].wait()
@@ -140,11 +163,31 @@
 
     lax.fori_loop(0, inner // q_tile, query_step, 0)
 
+    split = tile_of(width, 64)
+    half_way = width // split // 2
+
+    def split_step(i, carry):
+        at = pl.ds(pl.multiple_of(i * split, split), split)
+        pairs = kv_pairs[at]
+        w_kv[0, at, :] = pairs[:, 0, :]
+        w_kv[1, at, :] = pairs[:, 1, :]
+        return carry
+
     loads[1].wait()
-    for k, peer in enumerate(peers):
-        gather_copy(peer, k, peer).wait_recv()
-    for k, peer in enumerate(peers):
-        gather_copy(me, k, peer).wait_send()
+    lax.fori_loop(0, half_way, split_step, 0)
+
+    for peer in line[::-1]:
+        gather_copy(peer, peer, peer).wait_recv()
+        gather_copy(peer, peer + 1 - 2 * (me % 2), pair).start()
+    loads[2].wait()
+    gather_copy(pair, pair, pair).wait_recv()
+    for peer in line[::-1]:
+        across = peer + 1 - 2 * (me % 2)
+        gather_copy(across, across, pair).wait_recv()
+    for peer in line:
+        gather_copy(me, peer, peer).wait_send()
+        gather_copy(peer, peer + 1 - 2 * (me % 2), pair).wait_send()
+    gather_copy(me, pair, pair).wait_send()
 
     normed = normed_all[...].reshape(n * rows, width)
     h_tile = tile_of(hidden_count, 512)
@@ -156,7 +199,7 @@
         return carry
 
     lax.fori_loop(0, hidden_count // h_tile, hidden_step, 0)
-    loads[2].wait()
+    loads[3].wait()
 
     def sum_copy(c, source, k, peer):
         return to_peer(
@@ -175,6 +218,8 @@
 
     lax.fori_loop(0, chunks1, out_step, 0)
 
+    lax.fori_loop(half_way, width // split, split_step, 0)
+
     for c in range(chunks1):
         at = slice(c * chunk1, (c + 1) * chunk1)
         total = part[c, me]
@@ -184,9 +229,9 @@
         encoded_ref[:, at] = (tokens_ref[:, at].astype(F32) + total).astype(BF16)
     memory_all[0, me] = norm_rows(encoded_ref[...], final_gain_ref[...]).astype(BF16)
 
-    def memory_copy(source, k, peer):
+    def memory_copy(source, slot, peer):
         return to_peer(
-            memory_all.at[0, source], memory_all.at[0, source], mem_send.at[k], mem_recv.at[source], peer
+            memory_all.at[0, source], memory_all.at[0, source], mem_send.at[slot], mem_recv.at[source], peer
         )
 
     def forward_copy(source, s, other):
@@ -195,14 +240,14 @@
             fwd_send.at[s - 1, source], fwd_recv.at[cores - s - 1, source], other,
         )
 
-    for k, peer in enumerate(peers):
-        memory_copy(me, k, peer).start()
+    for peer in line:
+        memory_copy(me, peer, peer).start()
+    memory_copy(me, pair, pair).start()
     for s, other in enumerate(others, 1):
         forward_copy(me, s, other).start()
     for c in range(chunks1):
         for k, peer in enumerate(peers):
             sum_copy(c, me, k, peer).wait_send()
-    loads[3].wait()
     loads[4].wait()
 
     half = n * rows
@@ -226,10 +271,16 @@
     token_key = jnp.where(token % P_SLOT < token_length, token_owner, -1)
     allowed = token_key == question
 
-    for k, peer in enumerate(peers):
-        memory_copy(peer, k, peer).wait_recv()
+    for peer in line[::-1]:
+        memory_copy(peer, peer, peer).wait_recv()
+        memory_copy(peer, peer + 1 - 2 * (me % 2), pair).start()
         for s, other in enumerate(others, 1):
             forward_copy(peer, s, other).start()
+    for peer in [me] + line[::-1]:
+        across = peer + 1 - 2 * (me % 2)
+        memory_copy(across, across, pair).wait_recv()
+        for s, other in enumerate(others, 1):
+            forward_copy(across, s, other).start()
 
     k_tile = tile_of(inner, 512)
 
@@ -268,34 +319,55 @@
         summed = jnp.dot(weights.astype(BF16), head_values, preferred_element_type=F32)
         context[:, at] = (summed / total).astype(BF16)
 
-    def sum2_copy(c, source, k, peer):
-        return to_peer(
-            send2.at[c, peer], recv2.at[c, source], rs2_send.at[c, k], rs2_recv.at[c, source], peer
-        )
-
-    for c in range(chunks2):
-        product = jnp.dot(
-            context[...], w_proj[:, c * chunk2 : (c + 1) * chunk2], preferred_element_type=F32
-        )
-        for j in range(n):
-            block_rows = product[j * out_count : (j + 1) * out_count]
-            part2[c, j] = block_rows
-            send2[c, j] = block_rows.astype(BF16)
-        for k, peer in enumerate(peers):
-            sum2_copy(c, me, k, peer).start()
+    cut = width // cores
+
+    def columns_of(which):
+        return pl.ds(pl.multiple_of(which * cut, cut), cut)
+
+    def project_out(which):
+        return jnp.dot(context[...], w_proj[:, columns_of(which)], preferred_element_type=F32)
+
+    def core_copy(s, other):
+        return to_core(
+            pre_send.at[s - 1], pre_recv.at[cores - s - 1], pre_ssem.at[s - 1], pre_rsem.at[cores - s - 1], other
+        )
+
+    for s, other in enumerate(others, 1):
+        pre_send[s - 1] = project_out(other).astype(BF16)
+        core_copy(s, other).start()
+    product = project_out(core)
+    for s, other in enumerate(others, 1):
+        pltpu.make_async_remote_copy(
+            src_ref=pre_send.at[s - 1], dst_ref=pre_recv.at[s - 1],
+            send_sem=pre_ssem.at[s - 1], recv_sem=pre_rsem.at[s - 1],
+            device_id={"psg": other}, device_id_type=MESH,
+        ).wait_recv()
+        product = product + pre_recv[s - 1].astype(F32)
+    for j in range(n):
+        block_rows = product[j * out_count : (j + 1) * out_count]
+        part2[j] = block_rows
+        send2[j] = block_rows.astype(BF16)
+
+    def sum2_copy(source, k, peer):
+        return to_peer(send2.at[peer], recv2.at[source], rs2_send.at[k], rs2_recv.at[source], peer)
 
     for k, peer in enumerate(peers):
-        memory_copy(me, k, peer).wait_send()
+        sum2_copy(me, k, peer).start()
+
+    for peer in line:
+        memory_copy(me, peer, peer).wait_send()
+        memory_copy(peer, peer + 1 - 2 * (me % 2), pair).wait_send()
+    memory_copy(me, pair, pair).wait_send()
     for s, other in enumerate(others, 1):
         for source in [me] + peers:
             forward_copy(source, s, other).wait_send()
 
-    for c in range(chunks2):
-        total = part2[c, me]
-        for k, peer in enumerate(peers):
-            sum2_copy(c, peer, k, peer).wait_recv()
-            total = total + recv2[c, peer].astype(F32)
-        final_all[0, :, c * chunk2 : (c + 1) * chunk2] = total
+    total = part2[me]
+    for k, peer in list(enumerate(peers))[::-1]:
+        sum2_copy(peer, k, peer).wait_recv()
+        total = total + recv2[peer].astype(F32)
+    mine = columns_of(core)
+    final_all[0] = (own_answers_ref[me, :, mine].astype(F32) + total).astype(BF16)
 
     def final_copy(s, other):
         return to_core(
@@ -304,20 +376,24 @@
 
     for s, other in enumerate(others, 1):
         final_copy(s, other).start()
-    for c in range(chunks2):
-        for k, peer in enumerate(peers):
-            sum2_copy(c, me, k, peer).wait_send()
-    total = final_all[0]
-    for s, other in enumerate(others, 1):
+    answer_ref[:, mine] = final_all[0]
+    for k, peer in enumerate(peers):
+        sum2_copy(me, k, peer).wait_send()
+    for s, other in enumerate(others, 1):
+        core_copy(s, other).wait_send()
         pltpu.make_async_remote_copy(
             src_ref=final_all.at[0], dst_ref=final_all.at[s],
             send_sem=fin_send.at[s - 1], recv_sem=fin_recv.at[s - 1],
             device_id={"psg": other}, device_id_type=MESH,
         ).wait_recv()
-        total = total + final_all[s]
-    answer_ref[...] = (own_answers_ref[me].astype(F32) + total).astype(BF16)
+        answer_ref[:, columns_of(other)] = final_all[s]
     for s, other in enumerate(others, 1):
         final_copy(s, other).wait_send()
+
+
+def hand_over(encoded_in, answer_in, encoded_ref, answer_ref):
+    encoded_ref[...] = encoded_in[...]
+    answer_ref[...] = answer_in[...]
 
 
 def per_device(
@@ -344,16 +420,14 @@
     out_count = answer_count // n
     half = n * rows
     chunk1 = tile_of(width, 256)
-    chunk2 = tile_of(width, 512)
-    chunks1, chunks2 = width // chunk1, width // chunk2
-    core = lax.axis_index("psg")
-    w_kv = lax.dynamic_slice_in_dim(w_keyval, core * inner, inner, 2).transpose(1, 0, 2)
+    chunks1 = width // chunk1
+    cut = width // cores
     vmem = pl.BlockSpec(memory_space=pltpu.VMEM)
     smem = pl.BlockSpec(memory_space=pltpu.SMEM)
     hbm = pl.BlockSpec(memory_space=pl.ANY)
     dma = pltpu.SemaphoreType.DMA
     others = max(cores - 1, 1)
-    return pl.pallas_call(
+    encoded, answer = pl.pallas_call(
         functools.partial(kernel, n, cores),
         out_shape=(
             jax.ShapeDtypeStruct((rows, width), BF16),
@@ -364,6 +438,7 @@
         scratch_shapes=[
             pltpu.VMEM((width, hidden_count), BF16),
             pltpu.VMEM((hidden_count, width), BF16),
+            pltpu.VMEM((width, 2, inner), BF16),
             pltpu.VMEM((2, width, inner), BF16),
             pltpu.VMEM((width, inner), BF16),
             pltpu.VMEM((inner, width), BF16),
@@ -377,10 +452,12 @@
             pltpu.VMEM((cores, half, inner), BF16),
             pltpu.VMEM((answer_count, inner), BF16),
             pltpu.VMEM((answer_count, inner), BF16),
-            pltpu.VMEM((chunks2, n, out_count, chunk2), F32),
-            pltpu.VMEM((chunks2, n, out_count, chunk2), BF16),
-            pltpu.VMEM((chunks2, n, out_count, chunk2), BF16),
-            pltpu.VMEM((cores, out_count, width), F32),
+            pltpu.VMEM((others, answer_count, cut), BF16),
+            pltpu.VMEM((others, answer_count, cut), BF16),
+            pltpu.VMEM((n, out_count, cut), F32),
+            pltpu.VMEM((n, out_count, cut), BF16),
+            pltpu.VMEM((n, out_count, cut), BF16),
+            pltpu.VMEM((cores, out_count, cut), BF16),
             dma((5,)),
             dma((n,)),
             dma((n,)),
@@ -390,8 +467,10 @@
             dma((n,)),
             dma((others, n)),
             dma((others, n)),
-            dma((chunks2, n)),
-            dma((chunks2, n)),
+            dma((others,)),
+            dma((others,)),
+            dma((n,)),
+            dma((n,)),
             dma((others,)),
             dma((others,)),
         ],
@@ -410,10 +489,19 @@
         answer_lengths,
         w_in,
         w_out,
-        w_kv,
+        w_keyval,
         w_query,
         w_attn_out,
     )
+    return pl.pallas_call(
+        hand_over,
+        out_shape=(
+            jax.ShapeDtypeStruct(encoded.shape, BF16),
+            jax.ShapeDtypeStruct(answer.shape, BF16),
+        ),
+        in_specs=[vmem, vmem],
+        out_specs=(vmem, vmem),
+    )(encoded, answer)
 
 
 def solution(mesh):

time: 56.6 us -> 47.6 us (0.84)
  local copies, waits for them, and re-layouts: 11.1 us -> 0 us
  Pallas kernels: 44.5 us -> 46.7 us
    unnamed x3 -> x0, local copies, waits for them, and re-layouts: 6 us -> none
    dynamic_slice x1 -> x0, local copies, waits for them, and re-layouts: 5.07 us -> none  [per_device(): lax.dynamic_slice_in_dim(w_keyval, core * inner, inner, 2)]
    pallas_call x0 -> x1, Pallas kernels: none -> 1.4 us  [per_device(): pl.pallas_call(hand_over, out_shape=(jax.ShapeDtypeStruct(encoded.shape,...]
    pallas_call x1, Pallas kernels: 44.5 us -> 45.3 us  [per_device(): pl.pallas_call(functools.partial(kernel, n, cores), out_shape=(jax.ShapeD...]
where the time goes in v2:
time: 47.6 us; the launch traced here: 47.4 us
  Pallas kernels  46.7 us (98%)
  between operations  0.64 us (1%)
    pallas_call x1, Pallas kernels, per_device(): pl.pallas_call(functools.partial(kernel, n, cores), out_shape=(jax.ShapeD...  45.3 us
    pallas_call x1, Pallas kernels, per_device(): pl.pallas_call(hand_over, out_shape=(jax.ShapeDtypeStruct(encoded.shape,...  1.4 us

profile of v2, /device:TPU:0, one launch (start us, length us, event | category | flops | bytes accessed | tf_op | source)
XLA Modules:
  0.0 47.4 jit_solution(8290545526405556447)
XLA Ops:
  0.6 45.3 %shard_map.140 = (bf16[16,1024]{1,0:T(8,128)(2,1)}, bf16[16,1024]{1,0:T(8,128)(2,1)}) custom-call(bf16[16,1024]{1,0:T(8,128)(2,1)} %tokens_ref.1, f32[1,1024]{1,0:T(1,128)} %bitcast.5, f32[1,1024]{1,0:T(1,128)} %bitcast.6, f32[1,1024]{1,0:T(1,128)} %bitcast.7, bf16[128,1024]{1,0:T(8,128)(2,1)} %answers_ref.1, bf16[8,16,1024]{2,1,0:T(8,128)(2,1)} %bitcast.4, ...), custom_call_target="tpu_custom_call" | custom-call | tf_op jit(solution)/shard_map/pallas_call | solution.py:430
  46.0 1.4 %shard_map.141 = (bf16[16,1024]{1,0:T(8,128)(2,1)}, bf16[16,1024]{1,0:T(8,128)(2,1)}) custom-call(bf16[16,1024]{1,0:T(8,128)(2,1)} %get-tuple-element.4.encoded_in, bf16[16,1024]{1,0:T(8,128)(2,1)} %get-tuple-element.5.answer_in), custom_call_target="tpu_custom_call" | custom-call | tf_op jit(solution)/shard_map/pallas_call | solution.py:496

commit v3 on v1

--- a/solution.py
+++ b/solution.py
@@ -26,6 +26,22 @@
     while width % tile:
         tile //= 2
     return tile
+
+
+def flipped(index, mask):
+    out, bit = index, 1
+    while bit <= mask:
+        if mask & bit:
+            out = out + bit * (1 - 2 * ((index // bit) % 2))
+        bit *= 2
+    return out
+
+
+def peers_of(index, count):
+    if count & (count - 1):
+        return [lax.rem(index + k, count) for k in range(1, count)]
+    order = sorted(range(1, count), key=lambda k: (-(k.bit_length()), k))
+    return [flipped(index, k) for k in order]
 
 
 def kernel(
@@ -49,6 +65,7 @@
     answer_ref,
     w_in,
     w_out,
+    kv_pairs,
     w_kv,
     w_query,
     w_proj,
@@ -93,16 +110,16 @@
     first = pl.multiple_of(core * inner, inner)
     loads = [
         pltpu.make_async_copy(w_query_hbm.at[:, pl.ds(first, inner)], w_query, load_sem.at[0]),
+        pltpu.make_async_copy(w_kv_hbm.at[:, :, pl.ds(first, inner)], kv_pairs, load_sem.at[3]),
         pltpu.make_async_copy(w_in_hbm, w_in, load_sem.at[1]),
         pltpu.make_async_copy(w_out_hbm, w_out, load_sem.at[2]),
-        pltpu.make_async_copy(w_kv_hbm, w_kv, load_sem.at[3]),
         pltpu.make_async_copy(w_proj_hbm.at[pl.ds(first, inner), :], w_proj, load_sem.at[4]),
     ]
     for load in loads:
         load.start()
 
     barrier = pltpu.get_barrier_semaphore()
-    peers = [lax.rem(me + k, n) for k in range(1, n)]
+    peers = peers_of(me, n)
     others = [lax.rem(core + k, cores) for k in range(1, cores)]
     for peer in peers:
         pl.semaphore_signal(barrier, inc=1, device_id={"mp": peer}, device_id_type=MESH)
@@ -140,7 +157,20 @@
 
     lax.fori_loop(0, inner // q_tile, query_step, 0)
 
+    split = tile_of(width, 64)
+    half_way = width // split // 2
+
+    def split_step(i, carry):
+        at = pl.ds(pl.multiple_of(i * split, split), split)
+        pairs = kv_pairs[at]
+        w_kv[0, at, :] = pairs[:, 0, :]
+        w_kv[1, at, :] = pairs[:, 1, :]
+        return carry
+
     loads[1].wait()
+    lax.fori_loop(0, half_way, split_step, 0)
+
+    loads[2].wait()
     for k, peer in enumerate(peers):
         gather_copy(peer, k, peer).wait_recv()
     for k, peer in enumerate(peers):
@@ -156,7 +186,7 @@
         return carry
 
     lax.fori_loop(0, hidden_count // h_tile, hidden_step, 0)
-    loads[2].wait()
+    loads[3].wait()
 
     def sum_copy(c, source, k, peer):
         return to_peer(
@@ -175,6 +205,8 @@
 
     lax.fori_loop(0, chunks1, out_step, 0)
 
+    lax.fori_loop(half_way, width // split, split_step, 0)
+
     for c in range(chunks1):
         at = slice(c * chunk1, (c + 1) * chunk1)
         total = part[c, me]
@@ -202,7 +234,6 @@
     for c in range(chunks1):
         for k, peer in enumerate(peers):
             sum_copy(c, me, k, peer).wait_send()
-    loads[3].wait()
     loads[4].wait()
 
     half = n * rows
@@ -318,6 +349,11 @@
     answer_ref[...] = (own_answers_ref[me].astype(F32) + total).astype(BF16)
     for s, other in enumerate(others, 1):
         final_copy(s, other).wait_send()
+
+
+def hand_over(encoded_in, answer_in, encoded_ref, answer_ref):
+    encoded_ref[...] = encoded_in[...]
+    answer_ref[...] = answer_in[...]
 
 
 def per_device(
@@ -343,17 +379,15 @@
     answer_count = answer_states.shape[0]
     out_count = answer_count // n
     half = n * rows
-    chunk1 = tile_of(width, 256)
+    chunk1 = tile_of(width, 512)
     chunk2 = tile_of(width, 512)
     chunks1, chunks2 = width // chunk1, width // chunk2
-    core = lax.axis_index("psg")
-    w_kv = lax.dynamic_slice_in_dim(w_keyval, core * inner, inner, 2).transpose(1, 0, 2)
     vmem = pl.BlockSpec(memory_space=pltpu.VMEM)
     smem = pl.BlockSpec(memory_space=pltpu.SMEM)
     hbm = pl.BlockSpec(memory_space=pl.ANY)
     dma = pltpu.SemaphoreType.DMA
     others = max(cores - 1, 1)
-    return pl.pallas_call(
+    encoded, answer = pl.pallas_call(
         functools.partial(kernel, n, cores),
         out_shape=(
             jax.ShapeDtypeStruct((rows, width), BF16),
@@ -364,6 +398,7 @@
         scratch_shapes=[
             pltpu.VMEM((width, hidden_count), BF16),
             pltpu.VMEM((hidden_count, width), BF16),
+            pltpu.VMEM((width, 2, inner), BF16),
             pltpu.VMEM((2, width, inner), BF16),
             pltpu.VMEM((width, inner), BF16),
             pltpu.VMEM((inner, width), BF16),
@@ -410,10 +445,19 @@
         answer_lengths,
         w_in,
         w_out,
-        w_kv,
+        w_keyval,
         w_query,
         w_attn_out,
     )
+    return pl.pallas_call(
+        hand_over,
+        out_shape=(
+            jax.ShapeDtypeStruct(encoded.shape, BF16),
+            jax.ShapeDtypeStruct(answer.shape, BF16),
+        ),
+        in_specs=[vmem, vmem],
+        out_specs=(vmem, vmem),
+    )(encoded, answer)
 
 
 def solution(mesh):

time: 56.6 us -> 46.6 us (0.82)
  local copies, waits for them, and re-layouts: 11.1 us -> 0 us
  Pallas kernels: 44.5 us -> 45.8 us
    unnamed x3 -> x0, local copies, waits for them, and re-layouts: 6 us -> none
    dynamic_slice x1 -> x0, local copies, waits for them, and re-layouts: 5.07 us -> none  [per_device(): lax.dynamic_slice_in_dim(w_keyval, core * inner, inner, 2)]
    pallas_call x0 -> x1, Pallas kernels: none -> 1.4 us  [per_device(): pl.pallas_call(hand_over, out_shape=(jax.ShapeDtypeStruct(encoded.shape,...]
where the time goes in v3:
time: 46.6 us; the launch traced here: 46.4 us
  Pallas kernels  45.8 us (98%)
  between operations  0.64 us (1%)
    pallas_call x1, Pallas kernels, per_device(): pl.pallas_call(functools.partial(kernel, n, cores), out_shape=(jax.ShapeD...  44.4 us
    pallas_call x1, Pallas kernels, per_device(): pl.pallas_call(hand_over, out_shape=(jax.ShapeDtypeStruct(encoded.shape,...  1.4 us

profile of v3, /device:TPU:0, one launch (start us, length us, event | category | flops | bytes accessed | tf_op | source)
XLA Modules:
  0.0 46.4 jit_solution(14800386022026724121)
XLA Ops:
  0.6 44.4 %shard_map.140 = (bf16[16,1024]{1,0:T(8,128)(2,1)}, bf16[16,1024]{1,0:T(8,128)(2,1)}) custom-call(bf16[16,1024]{1,0:T(8,128)(2,1)} %tokens_ref.1, f32[1,1024]{1,0:T(1,128)} %bitcast.5, f32[1,1024]{1,0:T(1,128)} %bitcast.6, f32[1,1024]{1,0:T(1,128)} %bitcast.7, bf16[128,1024]{1,0:T(8,128)(2,1)} %answers_ref.1, bf16[8,16,1024]{2,1,0:T(8,128)(2,1)} %bitcast.4, ...), custom_call_target="tpu_custom_call" | custom-call | tf_op jit(solution)/shard_map/pallas_call | solution.py:390
  45.0 1.4 %shard_map.141 = (bf16[16,1024]{1,0:T(8,128)(2,1)}, bf16[16,1024]{1,0:T(8,128)(2,1)}) custom-call(bf16[16,1024]{1,0:T(8,128)(2,1)} %get-tuple-element.4.encoded_in, bf16[16,1024]{1,0:T(8,128)(2,1)} %get-tuple-element.5.answer_in), custom_call_target="tpu_custom_call" | custom-call | tf_op jit(solution)/shard_map/pallas_call | solution.py:452
